TPU v7x, 32 devices: a whole 2x2x4 slice. The times are simulated.
32 devices in a mesh: seq: 2 (over y), row: 4 (over x, core), rep: 4 (over z).
Axes of the slice: x: 2, y: 2, z: 4, core: 2. Of those that a mesh axis runs over, the one named last changes fastest.
Arguments:
- block_input: bfloat16 [4, 2048, 2048], P('row', 'seq', 'rep'), may hold values from -6 to 6
- cotangent: bfloat16 [4, 2048, 2048], P('row', 'seq', 'rep'), may hold values from -6 to 6
- segment_ids: int32 [4, 2048], P('row', 'seq'), may hold values from 0 to 3, never falling along the last dimension, each value on 1 to 1024 neighbouring positions
- pad_mask: int32 [4, 2048], P('row', 'seq'), may hold values 0 or 1
- state_init: float32 [4, 2816], P('row', 'rep'), may hold values from -6 to 6
- window_init: bfloat16 [4, 3, 2816], P('row', None, 'rep'), may hold values from -6 to 6
- recur_input: bfloat16 [2048, 2816], P(('seq', 'row'), 'rep'), may hold values from -0.125 to 0.125
- recur_gate: bfloat16 [2048, 2816], P(('seq', 'row'), 'rep'), may hold values from -0.125 to 0.125
- recur_output: bfloat16 [2048, 2816], P(('seq', 'row'), 'rep'), may hold values from -0.3125 to 0.3125
- feed_gate: bfloat16 [2048, 6144], P(('seq', 'row'), 'rep'), may hold values from -0.125 to 0.125
- feed_up: bfloat16 [2048, 6144], P(('seq', 'row'), 'rep'), may hold values from -0.125 to 0.125
- feed_down: bfloat16 [2048, 6144], P(('seq', 'row'), 'rep'), may hold values from -0.15625 to 0.15625
- conv_kernel: float32 [4, 2816], P(None, 'rep'), may hold values from -3 to 3
- conv_bias: float32 [2816], P('rep'), may hold values from -3 to 3
- decay_gate: bfloat16 [16, 176, 176], P('rep'), may hold values from -0.4375 to 0.4375
- input_gate: bfloat16 [16, 176, 176], P('rep'), may hold values from -0.4375 to 0.4375
- decay_bias: float32 [2816], P('rep'), may hold values from -4 to 4
- input_bias: float32 [2816], P('rep'), may hold values from -4 to 4
- decay_logit: float32 [2816], P('rep'), may hold values from -10.5 to -4.5
- mixer_gain: float32 [2048], replicated, may hold values from 0.25 to 1.75
- feed_gain: float32 [2048], replicated, may hold values from 0.25 to 1.75
Outputs:
- block_output: bfloat16 [4, 2048, 2048], P('row', 'seq', 'rep')
- block_states: float32 [4, 2, 2816], P('row', 'seq', 'rep')
- block_windows: bfloat16 [4, 2, 3, 2816], P('row', 'seq', None, 'rep')
- input_grad: bfloat16 [4, 2048, 2048], P('row', 'seq', 'rep')
- recur_input_grad: float32 [2048, 2816], P(('seq', 'row'), 'rep')
- recur_gate_grad: float32 [2048, 2816], P(('seq', 'row'), 'rep')
- recur_output_grad: float32 [2048, 2816], P(('seq', 'row'), 'rep')
- feed_gate_grad: float32 [2048, 6144], P(('seq', 'row'), 'rep')
- feed_up_grad: float32 [2048, 6144], P(('seq', 'row'), 'rep')
- feed_down_grad: float32 [2048, 6144], P(('seq', 'row'), 'rep')
- conv_kernel_grad: float32 [4, 2816], P(None, 'rep')
- conv_bias_grad: float32 [2816], P('rep')
- decay_gate_grad: float32 [16, 176, 176], P('rep')
- input_gate_grad: float32 [16, 176, 176], P('rep')
- decay_bias_grad: float32 [2816], P('rep')
- input_bias_grad: float32 [2816], P('rep')
- decay_logit_grad: float32 [2816], P('rep')
- mixer_gain_grad: float32 [2048], replicated
- feed_gain_grad: float32 [2048], replicated
Inputs may be any that keep to these rules, and one draw needn't show every extreme that they name: `segment_ids`: document numbers never fall along a row; each row holds 4 documents of at most 1024 positions.
All inputs are finite; a program needn't handle non-finite values. No bound on the sum of `pad_mask` on one device may be relied on, other than what follows from the above.
Results may differ from a plain program's by a relative error of at most 0.01.
Values may be sent and summed in bfloat16 or wider, within the bound.
A program may use at most 384 MiB of HBM per device.

v0:
```python
from functools import partial
import jax
import jax.numpy as jnp
from jax import lax
from jax.sharding import PartitionSpec as P

eps = 1e-06


def shifted_2(block, axis, distance):
    devices = range(lax.axis_size(axis))
    route = [(i - distance, i) for i in devices if i - distance in devices]
    return lax.ppermute(block, axis, route)


def entering(value, axis, join, neutral, backward):
    count, mine = (lax.axis_size(axis), lax.axis_index(axis))
    pieces = jax.tree.map(lambda part: lax.all_gather(part, axis), value)
    if backward:
        pieces = jax.tree.map(lambda part: part[::-1], pieces)
        mine = count - 1 - mine
    subtotal = jax.tree.map(
        lambda part, zero: jnp.full_like(part, 0) + jnp.asarray(zero, part.dtype), value, neutral
    )

    def hop(position, subtotal):
        longer = join(subtotal, jax.tree.map(lambda part: part[position], pieces))
        return jax.tree.map(lambda new, old: jnp.where(position < mine, new, old), longer, subtotal)

    return lax.fori_loop(0, count - 1, hop, subtotal)


def rms_norm(values, scales):
    return values * lax.rsqrt(jnp.mean(values * values, axis=-1, keepdims=True) + eps) * scales


def affine(former, latter):
    return (former[0] * latter[0], latter[0] * former[1] + latter[1])


def conv_math(padded, kernel, offset_bias, same_masks):
    tap_count = kernel.shape[0]
    length = padded.shape[1] - tap_count + 1
    total = offset_bias
    for offset in range(tap_count):
        start = tap_count - 1 - offset
        total = (
            total
            + kernel[offset] * padded[:, start : start + length] * same_masks[offset][..., None]
        )
    return total


def gate_math(conv_out, decay_pre, input_pre, decay_logit, retain_mask):
    rate_scale = 8.0 * jax.nn.softplus(decay_logit)
    exponent = rate_scale * jax.nn.sigmoid(decay_pre)
    retain = retain_mask[..., None] * jnp.exp(-exponent)
    inflow = jnp.sqrt(-jnp.expm1(-2.0 * exponent)) * jax.nn.sigmoid(input_pre) * conv_out
    return (retain, inflow)


def output_gate(hidden, gate_branch):
    return hidden * jax.nn.gelu(gate_branch, approximate=True)


def feed_math(gate_pre, up_pre):
    return jax.nn.gelu(gate_pre, approximate=True) * up_pre


def contract_last(left, right):
    return lax.dot_general(
        left, right, (((2,), (1,)), ((), ())), preferred_element_type=jnp.float32
    )


def outer_sum(left, right):
    return jnp.einsum("rtd,rtm->dm", left, right, preferred_element_type=jnp.float32)


def split_heads(values, head_count):
    return values.reshape(
        values.shape[0], values.shape[1], head_count, values.shape[2] // head_count
    )


def block_apply(values, blocks):
    row_count, length, channels = values.shape
    heads_in = split_heads(values, blocks.shape[0])
    mixed = jnp.einsum("rthi,hij->rthj", heads_in, blocks, preferred_element_type=jnp.float32)
    return mixed.reshape(row_count, length, channels)


def block_apply_back(grads, blocks):
    row_count, length, channels = grads.shape
    heads_in = split_heads(grads, blocks.shape[0])
    mixed = jnp.einsum("rthj,hij->rthi", heads_in, blocks, preferred_element_type=jnp.float32)
    return mixed.reshape(row_count, length, channels)


def block_outer(values, grads, head_count):
    return jnp.einsum(
        "rthi,rthj->hij",
        split_heads(values, head_count),
        split_heads(grads, head_count),
        preferred_element_type=jnp.float32,
    )


def shards(
    block_input,
    cotangent,
    segment_ids,
    pad_mask,
    state_init,
    window_init,
    recur_input,
    recur_gate,
    recur_output,
    feed_gate,
    feed_up,
    feed_down,
    conv_kernel,
    conv_bias,
    decay_gate,
    input_gate,
    decay_bias,
    input_bias,
    decay_logit,
    mixer_gain,
    feed_gain,
):
    own_width = block_input.shape[2]
    rep_index = lax.axis_index("rep")
    at_start = lax.axis_index("seq") == 0
    head_count = decay_gate.shape[0]
    tap_count = conv_kernel.shape[0]
    edge_width = tap_count - 1
    length = segment_ids.shape[1]
    masked_low = cotangent * pad_mask[..., None].astype(jnp.bfloat16)
    whole_input, whole_masked = (
        lax.all_gather(block_input, "rep", axis=2, tiled=True),
        lax.all_gather(masked_low, "rep", axis=2, tiled=True),
    )
    fetched = (
        lax.all_gather(recur_input, ("seq", "row"), axis=0, tiled=True),
        lax.all_gather(recur_gate, ("seq", "row"), axis=0, tiled=True),
        lax.all_gather(recur_output, ("seq", "row"), axis=0, tiled=True),
        lax.all_gather(feed_gate, ("seq", "row"), axis=0, tiled=True),
        lax.all_gather(feed_up, ("seq", "row"), axis=0, tiled=True),
        lax.all_gather(feed_down, ("seq", "row"), axis=0, tiled=True),
    )
    input_float = whole_input.astype(jnp.float32)
    normed_f, norm_one_back = jax.vjp(rms_norm, input_float, mixer_gain)
    normed = normed_f.astype(jnp.bfloat16)
    conv_input = jnp.dot(normed, fetched[0], preferred_element_type=jnp.float32).astype(
        jnp.bfloat16
    )
    gate_branch = jnp.dot(normed, fetched[1], preferred_element_type=jnp.float32)
    left_input, left_marks = shifted_2(
        (conv_input[:, -edge_width:], segment_ids[:, -edge_width:].astype(jnp.bfloat16)), "seq", 1
    )
    left_ids = left_marks.astype(jnp.int32)
    left_ids = jnp.where(at_start, jnp.broadcast_to(segment_ids[:, :1], left_ids.shape), left_ids)
    left_input = jnp.where(at_start, window_init, left_input)
    ids_ext = jnp.concatenate([left_ids, segment_ids], axis=1)
    same_masks = [
        (ids_ext[:, edge_width - offset : edge_width - offset + length] == segment_ids).astype(
            jnp.float32
        )
        for offset in range(tap_count)
    ]
    retain_mask = (ids_ext[:, edge_width - 1 : edge_width - 1 + length] == segment_ids).astype(
        jnp.float32
    )
    padded = jnp.concatenate([left_input, conv_input], axis=1).astype(jnp.float32)
    conv_out, conv_back = jax.vjp(
        partial(conv_math, same_masks=same_masks), padded, conv_kernel, conv_bias
    )
    conv_low = conv_out.astype(jnp.bfloat16)
    decay_pre = block_apply(conv_low, decay_gate) + decay_bias
    input_pre = block_apply(conv_low, input_gate) + input_bias
    (retain, inflow), gate_back = jax.vjp(
        partial(gate_math, retain_mask=retain_mask), conv_out, decay_pre, input_pre, decay_logit
    )
    products, partial_states = lax.associative_scan(affine, (retain, inflow), axis=1)
    carry_decay, carry_state = entering(
        (products[:, -1], partial_states[:, -1]),
        "seq",
        affine,
        (jnp.ones_like(state_init), jnp.zeros_like(state_init)),
        False,
    )
    state_in = carry_decay * state_init + carry_state
    hidden = partial_states + products * state_in[:, None]
    block_states = hidden[:, -1:]
    block_windows = conv_input[:, None, -edge_width:]
    gated_f, gated_back = jax.vjp(output_gate, hidden, gate_branch)
    gated = gated_f.astype(jnp.bfloat16)
    branch = lax.psum(contract_last(gated, fetched[2]), "rep")
    middle = input_float + branch
    normed_mid_f, norm_two_back = jax.vjp(rms_norm, middle, feed_gain)
    normed_mid = normed_mid_f.astype(jnp.bfloat16)
    gate_pre = jnp.dot(normed_mid, fetched[3], preferred_element_type=jnp.float32)
    up_pre = jnp.dot(normed_mid, fetched[4], preferred_element_type=jnp.float32)
    feed_f, feed_back = jax.vjp(feed_math, gate_pre, up_pre)
    feed_low = feed_f.astype(jnp.bfloat16)
    feed_out = lax.psum_scatter(
        contract_last(feed_low, fetched[5]), "rep", scatter_dimension=2, tiled=True
    )
    middle_own = lax.dynamic_slice_in_dim(middle, rep_index * own_width, own_width, 2)
    block_output = (middle_own + feed_out).astype(jnp.bfloat16)
    back_weights = (
        lax.all_gather(recur_input, ("seq", "row"), axis=0, tiled=True),
        lax.all_gather(recur_gate, ("seq", "row"), axis=0, tiled=True),
        lax.all_gather(recur_output, ("seq", "row"), axis=0, tiled=True),
        lax.all_gather(feed_gate, ("seq", "row"), axis=0, tiled=True),
        lax.all_gather(feed_up, ("seq", "row"), axis=0, tiled=True),
        lax.all_gather(feed_down, ("seq", "row"), axis=0, tiled=True),
    )
    grad_feed = jnp.dot(whole_masked, back_weights[5], preferred_element_type=jnp.float32)
    feed_down_grad = outer_sum(whole_masked, feed_low)
    gate_grad_f, up_grad_f = feed_back(grad_feed)
    gate_grad = gate_grad_f.astype(jnp.bfloat16)
    up_grad = up_grad_f.astype(jnp.bfloat16)
    feed_gate_grad = outer_sum(normed_mid, gate_grad)
    feed_up_grad = outer_sum(normed_mid, up_grad)
    mid_normed_grad = lax.psum(
        contract_last(gate_grad, back_weights[3]) + contract_last(up_grad, back_weights[4]), "rep"
    )
    middle_norm_grad, feed_gain_grad = norm_two_back(mid_normed_grad)
    middle_grad = whole_masked.astype(jnp.float32) + middle_norm_grad
    middle_low = middle_grad.astype(jnp.bfloat16)
    gated_grad = jnp.dot(middle_low, back_weights[2], preferred_element_type=jnp.float32)
    recur_output_grad = outer_sum(middle_low, gated)
    hidden_grad, branch_grad_f = gated_back(gated_grad)
    branch_grad = branch_grad_f.astype(jnp.bfloat16)
    shifted = jnp.concatenate([retain[:, 1:], jnp.ones_like(retain[:, :1])], axis=1)
    after_decay, local_adjoint = lax.associative_scan(
        affine, (shifted, hidden_grad), axis=1, reverse=True
    )
    carry_back = entering(
        (products[:, -1], retain[:, 0] * local_adjoint[:, 0]),
        "seq",
        affine,
        (jnp.ones_like(state_init), jnp.zeros_like(state_init)),
        True,
    )
    adjoint = local_adjoint + after_decay * carry_back[1][:, None]
    hidden_prev = jnp.concatenate([state_in[:, None], hidden[:, :-1]], axis=1)
    conv_direct, decay_pre_f, input_pre_f, decay_logit_grad = gate_back(
        (adjoint * hidden_prev, adjoint)
    )
    decay_pre_grad = decay_pre_f.astype(jnp.bfloat16)
    input_pre_grad = input_pre_f.astype(jnp.bfloat16)
    decay_gate_grad = block_outer(conv_low, decay_pre_grad, head_count)
    input_gate_grad = block_outer(conv_low, input_pre_grad, head_count)
    decay_bias_grad = jnp.sum(decay_pre_grad.astype(jnp.float32), axis=(0, 1))
    input_bias_grad = jnp.sum(input_pre_grad.astype(jnp.float32), axis=(0, 1))
    conv_grad = (
        conv_direct
        + block_apply_back(decay_pre_grad, decay_gate)
        + block_apply_back(input_pre_grad, input_gate)
    )
    padded_grad, conv_kernel_grad, conv_bias_grad = conv_back(conv_grad)
    from_right = shifted_2(padded_grad[:, :edge_width], "seq", -1)
    own_grad = padded_grad[:, edge_width:]
    own_grad = jnp.concatenate(
        [own_grad[:, :-edge_width], own_grad[:, -edge_width:] + from_right], axis=1
    )
    input_low_grad = own_grad.astype(jnp.bfloat16)
    recur_input_grad = outer_sum(normed, input_low_grad)
    recur_gate_grad = outer_sum(normed, branch_grad)
    normed_terms = contract_last(input_low_grad, back_weights[0]) + contract_last(
        branch_grad, back_weights[1]
    )
    middle_grad_own = lax.dynamic_slice_in_dim(middle_grad, rep_index * own_width, own_width, 2)
    normed_grad = lax.psum(normed_terms, "rep")
    input_norm_grad, mixer_gain_grad = norm_one_back(normed_grad)
    input_norm_own = lax.dynamic_slice_in_dim(input_norm_grad, rep_index * own_width, own_width, 2)
    input_grad = (middle_grad_own + input_norm_own).astype(jnp.bfloat16)
    matrix_grads = (
        lax.psum_scatter(recur_input_grad, ("seq", "row"), scatter_dimension=0, tiled=True),
        lax.psum_scatter(recur_gate_grad, ("seq", "row"), scatter_dimension=0, tiled=True),
        lax.psum_scatter(recur_output_grad, ("seq", "row"), scatter_dimension=0, tiled=True),
        lax.psum_scatter(feed_gate_grad, ("seq", "row"), scatter_dimension=0, tiled=True),
        lax.psum_scatter(feed_up_grad, ("seq", "row"), scatter_dimension=0, tiled=True),
        lax.psum_scatter(feed_down_grad, ("seq", "row"), scatter_dimension=0, tiled=True),
    )
    small_grads = lax.psum(
        (
            conv_kernel_grad,
            conv_bias_grad,
            decay_gate_grad,
            input_gate_grad,
            decay_bias_grad,
            input_bias_grad,
            decay_logit_grad,
            mixer_gain_grad,
            feed_gain_grad,
        ),
        ("seq", "row"),
    )
    return (
        block_output,
        block_states,
        block_windows,
        input_grad,
        matrix_grads[0],
        matrix_grads[1],
        matrix_grads[2],
        matrix_grads[3],
        matrix_grads[4],
        matrix_grads[5],
        small_grads[0],
        small_grads[1],
        small_grads[2],
        small_grads[3],
        small_grads[4],
        small_grads[5],
        small_grads[6],
        small_grads[7],
        small_grads[8],
    )


def solution(mesh):
    in_specs = (
        P("row", "seq", "rep"),
        P("row", "seq", "rep"),
        P("row", "seq"),
        P("row", "seq"),
        P("row", "rep"),
        P("row", None, "rep"),
        P(("seq", "row"), "rep"),
        P(("seq", "row"), "rep"),
        P(("seq", "row"), "rep"),
        P(("seq", "row"), "rep"),
        P(("seq", "row"), "rep"),
        P(("seq", "row"), "rep"),
        P(None, "rep"),
        P("rep"),
        P("rep", None, None),
        P("rep", None, None),
        P("rep"),
        P("rep"),
        P("rep"),
        P(),
        P(),
    )
    out_specs = (
        P("row", "seq", "rep"),
        P("row", "seq", "rep"),
        P("row", "seq", None, "rep"),
        P("row", "seq", "rep"),
        P(("seq", "row"), "rep"),
        P(("seq", "row"), "rep"),
        P(("seq", "row"), "rep"),
        P(("seq", "row"), "rep"),
        P(("seq", "row"), "rep"),
        P(("seq", "row"), "rep"),
        P(None, "rep"),
        P("rep"),
        P("rep", None, None),
        P("rep", None, None),
        P("rep"),
        P("rep"),
        P("rep"),
        P(),
        P(),
    )
    return jax.shard_map(shards, mesh=mesh, in_specs=in_specs, out_specs=out_specs, check_vma=False)
```

profile of v0, /device:TPU:0, one launch (start us, length us, event | category | flops | bytes accessed | tf_op | source)
XLA Modules:
  0.0 4679.4 jit_solution(15603391600166171410)
XLA Ops:
  20.5 72.6 %all-gather.9.cloned.1.call-done = bf16[1,1024,2048]{2,1,0:T(8,128)(2,1)} async-done(((bf16[1,1024,512]{2,1,0:T(8,128)(2,1)}), bf16[1,1024,2048]{2,1,0:T(8,128)(2,1)}) %all-gather.9.cloned.1.call-update) | async-done | bytes 4194320 | tf_op jit(solution)/shard_map/all_gather | solution.py:141
  96.2 29.0 all-gather.11.cloned.1.call-done
  135.3 27.0 all-gather.13.cloned.1.call-done
  181.9 50.8 %slice.699 = f32[1,512,704]{1,2,0:T(8,128)} slice(f32[1,1024,704]{1,2,0:T(8,128)S(1)} %get-tuple-element.180), slice={[0:1:1], [1:1024:2], [0:704:1]} | slice | bytes 2883584 | tf_op jit(solution)/shard_map/slice | solution.py:185
  232.7 50.7 %slice.703 = f32[1,512,704]{1,2,0:T(8,128)} slice(f32[1,1024,704]{1,2,0:T(8,128)S(1)} %get-tuple-element.180), slice={[0:1:1], [0:1023:2], [0:704:1]} | slice | bytes 2883584 | tf_op jit(solution)/shard_map/slice | solution.py:185
  283.5 51.4 %slice.700 = f32[1,512,704]{1,2,0:T(8,128)} slice(f32[1,1024,704]{1,2,0:T(8,128)} %get-tuple-element.181), slice={[0:1:1], [0:1023:2], [0:704:1]} | slice | bytes 2883584 | tf_op jit(solution)/shard_map/slice | solution.py:185
  334.9 51.3 %slice.701 = f32[1,512,704]{1,2,0:T(8,128)} slice(f32[1,1024,704]{1,2,0:T(8,128)} %get-tuple-element.181), slice={[0:1:1], [1:1024:2], [0:704:1]} | slice | bytes 2883584 | tf_op jit(solution)/shard_map/slice | solution.py:185
  391.1 28.3 slice.706
  419.4 28.3 slice.707
  447.7 28.5 slice.705
  476.2 28.3 slice.709
  541.2 17.2 slice.711
  795.7 28.2 slice.704
  823.9 28.6 slice.769
  856.0 50.7 %slice.698 = f32[1,511,704]{1,2,0:T(8,128)} slice(f32[1,1024,704]{1,2,0:T(8,128)S(1)} %get-tuple-element.180), slice={[0:1:1], [2:1024:2], [0:704:1]} | slice | bytes 2877952 | tf_op jit(solution)/shard_map/slice | solution.py:185
  906.7 51.2 %slice.771 = f32[1,511,704]{1,2,0:T(8,128)} slice(f32[1,1024,704]{1,2,0:T(8,128)} %get-tuple-element.181), slice={[0:1:1], [2:1024:2], [0:704:1]} | slice | bytes 2877952 | tf_op jit(solution)/shard_map/slice | solution.py:185
  1199.9 28.7 pad.306
  1228.6 28.9 pad.307
  1257.5 28.7 pad.287
  1288.5 28.6 pad.286
  1326.9 57.3 %pad.308 = f32[1,1024,704]{1,2,0:T(8,128)} pad(f32[1,512,704]{1,2,0:T(8,128)} %pad_maximum_fusion.1, f32[]{:T(128)} %constant.20.clone.1), padding=0_0_0x0_1_1x0_0_0 | pad | bytes 4325380 | tf_op jit(solution)/shard_map/pad | solution.py:185
  1384.2 57.2 %pad.309 = f32[1,1024,704]{1,2,0:T(8,128)} pad(f32[1,512,704]{1,2,0:T(8,128)} %add.770, f32[]{:T(128)} %constant.20.clone.1), padding=0_0_0x1_0_1x0_0_0 | pad | bytes 4325380 | tf_op jit(solution)/shard_map/pad | solution.py:185
  1447.5 57.1 %pad.288 = f32[1,1024,704]{1,2,0:T(8,128)} pad(f32[1,512,704]{1,2,0:T(8,128)} %pad_maximum_fusion, f32[]{:T(128)} %constant.20.clone.1), padding=0_0_0x0_1_1x0_0_0 | pad | bytes 4325380 | tf_op jit(solution)/shard_map/pad | solution.py:185
  1504.6 57.3 %pad.289 = f32[1,1024,704]{1,2,0:T(8,128)} pad(f32[1,512,704]{1,2,0:T(8,128)} %add.759, f32[]{:T(128)} %constant.20.clone.1), padding=0_0_0x1_0_1x0_0_0 | pad | bytes 4325380 | tf_op jit(solution)/shard_map/pad | solution.py:185
  1595.3 286.3 %all-reduce.97.cloned.1.call-done = f32[1,1024,2048]{2,1,0:T(8,128)} async-done(((f32[1,1024,2048]{2,1,0:T(8,128)}), f32[1,1024,2048]{2,1,0:T(8,128)}) %all-reduce.97.cloned.1.call-update) | async-done | bytes 8388624 | tf_op jit(solution)/shard_map/psum | solution.py:199
  1893.8 34.1 all-gather.17.cloned.1.call-done
  1939.8 35.6 all-gather.19.cloned.1.call-done
  1987.1 71.2 %all-gather.23.cloned.1.call-done = bf16[1,1024,2048]{2,1,0:T(8,128)(2,1)} async-done(((bf16[1,1024,512]{2,1,0:T(8,128)(2,1)}), bf16[1,1024,2048]{2,1,0:T(8,128)(2,1)}) %all-gather.23.cloned.1.call-update) | async-done | bytes 4194320 | tf_op jit(solution)/shard_map/all_gather | solution.py:142
  2058.3 46.0 all-gather.21.cloned.1.call-done
  2104.3 18.4 multiply_convert_fusion.2
  2146.4 51.2 %slice.798 = f32[1,512,704]{1,2,0:T(8,128)} slice(f32[1,1024,704]{1,2,0:T(8,128)} %concatenate.160), slice={[0:1:1], [0:1023:2], [0:704:1]} | slice | bytes 2883584 | tf_op jit(solution)/shard_map/slice | solution.py:238
  2197.7 51.3 %slice.805 = f32[1,512,704]{1,2,0:T(8,128)} slice(f32[1,1024,704]{1,2,0:T(8,128)} %concatenate.160), slice={[0:1:1], [1:1024:2], [0:704:1]} | slice | bytes 2883584 | tf_op jit(solution)/shard_map/slice | solution.py:238
  2249.0 51.3 %slice.796 = f32[1,511,704]{1,2,0:T(8,128)} slice(f32[1,1024,704]{1,2,0:T(8,128)} %concatenate.160), slice={[0:1:1], [1:1022:2], [0:704:1]} | slice | bytes 2877952 | tf_op jit(solution)/shard_map/slice | solution.py:238
  2352.8 81.8 %all-reduce.99.cloned.1.call-done = f32[1,1024,2048]{2,1,0:T(8,128)} async-done(((f32[1,1024,2048]{2,1,0:T(8,128)}), f32[1,1024,2048]{2,1,0:T(8,128)}) %all-reduce.99.cloned.1.call-update) | async-done | bytes 8388624 | tf_op jit(solution)/shard_map/psum | solution.py:227
  2462.4 51.3 %slice.800 = f32[1,512,704]{1,2,0:T(8,128)} slice(f32[1,1024,704]{1,2,0:T(8,128)} %multiply_bitcast_fusion), slice={[0:1:1], [1:1024:2], [0:704:1]} | slice | bytes 2883584 | tf_op jit(solution)/shard_map/slice | solution.py:238
  2513.7 51.4 %slice.802 = f32[1,512,704]{1,2,0:T(8,128)} slice(f32[1,1024,704]{1,2,0:T(8,128)} %multiply_bitcast_fusion), slice={[0:1:1], [0:1023:2], [0:704:1]} | slice | bytes 2883584 | tf_op jit(solution)/shard_map/slice | solution.py:238
  2596.6 28.3 slice.809
  2624.9 28.3 slice.810
  2653.2 28.3 slice.808
  2681.6 28.7 slice.812
  2763.8 17.0 slice.818
  2959.7 17.1 slice.813
  2997.0 28.2 slice.807
  3025.2 28.4 slice.872
  3057.2 51.3 %slice.874 = f32[1,511,704]{1,2,0:T(8,128)} slice(f32[1,1024,704]{1,2,0:T(8,128)} %multiply_bitcast_fusion), slice={[0:1:1], [1:1022:2], [0:704:1]} | slice | bytes 2877952 | tf_op jit(solution)/shard_map/slice | solution.py:238
  3355.0 28.7 pad.326
  3383.7 28.8 pad.327
  3415.7 57.2 %pad.329 = f32[1,1024,704]{1,2,0:T(8,128)} pad(f32[1,512,704]{1,2,0:T(8,128)} %add.812, f32[]{:T(128)} %constant.20.clone.1), padding=0_0_0x1_0_1x0_0_0 | pad | bytes 4325380 | tf_op jit(solution)/shard_map/pad | solution.py:238
  3475.1 28.6 pad.346
  3503.8 28.9 pad.347
  3554.7 57.2 %pad.328 = f32[1,1024,704]{1,2,0:T(8,128)} pad(f32[1,512,704]{1,2,0:T(8,128)} %pad_maximum_fusion.2, f32[]{:T(128)} %constant.20.clone.1), padding=0_0_0x0_1_1x0_0_0 | pad | bytes 4325380 | tf_op jit(solution)/shard_map/pad | solution.py:238
  3620.2 52.7 %pad.349 = f32[1,1024,704]{1,2,0:T(8,128)S(1)} pad(f32[1,512,704]{1,2,0:T(8,128)} %add.823, f32[]{:T(128)} %constant.20.clone.1), padding=0_0_0x1_0_1x0_0_0 | pad | bytes 4325380 | tf_op jit(solution)/shard_map/pad | solution.py:238
  3676.0 57.2 %pad.348 = f32[1,1024,704]{1,2,0:T(8,128)} pad(f32[1,512,704]{1,2,0:T(8,128)} %concatenate.178, f32[]{:T(128)} %constant.20.clone.1), padding=0_0_0x0_1_1x0_0_0 | pad | bytes 4325380 | tf_op jit(solution)/shard_map/pad | solution.py:238
  3737.2 25.7 rev.5
  3762.9 25.9 rev.4
  3924.4 204.8 %all-reduce.101.cloned.1.call-done = f32[1,1024,2048]{2,1,0:T(8,128)} async-done(((f32[1,1024,2048]{2,1,0:T(8,128)}), f32[1,1024,2048]{2,1,0:T(8,128)}) %all-reduce.101.cloned.1.call-update) | async-done | bytes 8388624 | tf_op jit(solution)/shard_map/psum | solution.py:277
  4137.4 25.4 all-reduce.90
  4167.2 23.5 all-reduce.103.cloned.1.call-done
  4190.7 62.5 %reduce-scatter.14.cloned.1.call-done = f32[256,704]{0,1:T(8,128)} async-done(((f32[2048,704]{0,1:T(8,128)}), f32[256,704]{0,1:T(8,128)}) %reduce-scatter.14.cloned.1.call-update) | async-done | bytes 720912 | tf_op jit(solution)/shard_map/reduce_scatter | solution.py:284
  4253.2 62.9 %reduce-scatter.12.cloned.1.call-done = f32[256,704]{0,1:T(8,128)} async-done(((f32[2048,704]{0,1:T(8,128)}), f32[256,704]{0,1:T(8,128)}) %reduce-scatter.12.cloned.1.call-update) | async-done | bytes 720912 | tf_op jit(solution)/shard_map/reduce_scatter | solution.py:283
  4316.2 63.3 %reduce-scatter.10.cloned.1.call-done = f32[256,704]{0,1:T(8,128)} async-done(((f32[2048,704]{0,1:T(8,128)}), f32[256,704]{0,1:T(8,128)}) %reduce-scatter.10.cloned.1.call-update) | async-done | bytes 720912 | tf_op jit(solution)/shard_map/reduce_scatter | solution.py:282
  4379.5 96.3 %reduce-scatter.16.cloned.1.call-done = f32[256,1536]{1,0:T(8,128)} async-done(((f32[2048,1536]{1,0:T(8,128)}), f32[256,1536]{1,0:T(8,128)}) %reduce-scatter.16.cloned.1.call-update) | async-done | bytes 1572880 | tf_op jit(solution)/shard_map/reduce_scatter | solution.py:285
  4475.8 96.4 %reduce-scatter.18.cloned.1.call-done = f32[256,1536]{1,0:T(8,128)} async-done(((f32[2048,1536]{1,0:T(8,128)}), f32[256,1536]{1,0:T(8,128)}) %reduce-scatter.18.cloned.1.call-update) | async-done | bytes 1572880 | tf_op jit(solution)/shard_map/reduce_scatter | solution.py:286
  4572.2 96.5 %reduce-scatter.20.cloned.1.call-done = f32[256,1536]{1,0:T(8,128)} async-done(((f32[2048,1536]{1,0:T(8,128)}), f32[256,1536]{1,0:T(8,128)}) %reduce-scatter.20.cloned.1.call-update) | async-done | bytes 1572880 | tf_op jit(solution)/shard_map/reduce_scatter | solution.py:287
  (642 shorter events, 1489.7 us)
Async XLA Ops:
  7.2 167.8 %copy-start = (bf16[4,176,176]{2,1,0:T(8,128)(2,1)S(1)}, bf16[4,176,176]{2,1,0:T(8,128)(2,1)}, u32[]{:S(2)}) copy-start(bf16[4,176,176]{2,1,0:T(8,128)(2,1)} %param.36) | copy-start | bytes 743428
  7.2 85.9 %all-gather.9.cloned.1.call-start = ((), (), s32[]{:S(2)}) async-start(), calls=%async_computation.7 | async-start | bytes 5242880 | tf_op jit(solution)/shard_map/all_gather | solution.py:141
  7.9 117.3 %copy-start.98 = (f32[2048]{0:T(1024)S(1)}, f32[2048]{0:T(1024)}, u32[]{:S(2)}) copy-start(f32[2048]{0:T(1024)} %param.40) | copy-start | bytes 24580
  8.0 117.3 %all-gather.11.cloned.1.call-start = ((), (), s32[]{:S(2)}) async-start(), calls=%async_computation.8 | async-start | bytes 3244032 | tf_op jit(solution)/shard_map/all_gather | solution.py:145
  8.7 153.6 %all-gather.13.cloned.1.call-start = ((), (), s32[]{:S(2)}) async-start(), calls=%async_computation.9 | async-start | bytes 3244032 | tf_op jit(solution)/shard_map/all_gather | solution.py:146
  9.4 1572.1 %all-gather.15.cloned.1.call-start = ((), (), s32[]{:S(2)}) async-start(), calls=%async_computation.10 | async-start | bytes 3244032 | tf_op jit(solution)/shard_map/all_gather | solution.py:147
  10.2 8.6 collective-permute-start.1
  15.1 1866.5 %all-reduce.97.cloned.1.call-start = ((), (), s32[]{:S(2)}) async-start(), calls=%async_computation.11 | async-start | bytes 16777216 | tf_op jit(solution)/shard_map/psum | solution.py:199
  18.1 153.1 %copy-start.84 = (f32[704]{0:T(1024)}, f32[704]{0:T(1024)S(1)}, u32[]{:S(2)}) copy-start(f32[704]{0:T(1024)S(1)} %get-tuple-element.143) | copy-start | bytes 8452
  18.1 153.1 %copy-start.86 = (f32[704]{0:T(1024)}, f32[704]{0:T(1024)S(1)}, u32[]{:S(2)}) copy-start(f32[704]{0:T(1024)S(1)} %get-tuple-element.144) | copy-start | bytes 8452
  18.1 153.1 %copy-start.88 = (f32[704]{0:T(1024)}, f32[704]{0:T(1024)S(1)}, u32[]{:S(2)}) copy-start(f32[704]{0:T(1024)S(1)} %get-tuple-element.145) | copy-start | bytes 8452
  18.1 153.0 %copy-start.90 = (f32[704]{0:T(1024)}, f32[704]{0:T(1024)S(1)}, u32[]{:S(2)}) copy-start(f32[704]{0:T(1024)S(1)} %get-tuple-element.146) | copy-start | bytes 8452
  18.8 158.0 %copy-start.71 = (f32[704]{0:T(1024)}, f32[704]{0:T(1024)S(1)}, u32[]{:S(2)}) copy-start(f32[704]{0:T(1024)S(1)} %fusion.79) | copy-start | bytes 8452
  20.5 150.7 %copy-start.78 = (f32[1,1024]{1,0:T(1,128)}, f32[1,1024]{1,0:T(1,128)S(1)}, u32[]{:S(2)}) copy-start(f32[1,1024]{1,0:T(1,128)S(1)} %get-tuple-element.273) | copy-start | bytes 12292
  20.5 150.7 %copy-start.80 = (f32[1,1024]{1,0:T(1,128)}, f32[1,1024]{1,0:T(1,128)S(1)}, u32[]{:S(2)}) copy-start(f32[1,1024]{1,0:T(1,128)S(1)} %get-tuple-element.274) | copy-start | bytes 12292
  20.5 156.4 %copy-start.69 = (f32[1,1024]{1,0:T(1,128)}, f32[1,1024]{1,0:T(1,128)S(1)}, u32[]{:S(2)}) copy-start(f32[1,1024]{1,0:T(1,128)S(1)} %get-tuple-element.272) | copy-start | bytes 12292
  96.2 35.4 copy-start.82
  96.2 66.1 %copy-start.92 = (f32[1024]{0:T(1024)}, f32[1024]{0:T(1024)S(1)}, u32[]{:S(2)}) copy-start(f32[1024]{0:T(1024)S(1)} %fusion.80) | copy-start | bytes 12292
  132.4 38.0 collective-permute-start
  1026.9 6.2 copy-start.33
  1051.9 6.2 copy-start.31
  1082.9 6.2 copy-start.29
  1125.7 6.1 copy-start.65
  1504.6 69.2 %copy-start.102 = (f32[1,704]{1,0:T(1,128)S(1)}, f32[1,704]{1,0:T(1,128)}, u32[]{:S(2)}) copy-start(f32[1,704]{1,0:T(1,128)} %param.25) | copy-start | bytes 8452
  1590.6 337.3 %all-gather.17.cloned.1.call-start = ((), (), s32[]{:S(2)}) async-start(), calls=%async_computation.12 | async-start | bytes 7077888 | tf_op jit(solution)/shard_map/all_gather | solution.py:148
  1591.2 384.1 %all-gather.19.cloned.1.call-start = ((), (), s32[]{:S(2)}) async-start(), calls=%async_computation.13 | async-start | bytes 7077888 | tf_op jit(solution)/shard_map/all_gather | solution.py:149
  1592.0 466.3 %all-gather.23.cloned.1.call-start = ((), (), s32[]{:S(2)}) async-start(), calls=%async_computation.16 | async-start | bytes 5242880 | tf_op jit(solution)/shard_map/all_gather | solution.py:142
  1594.5 509.8 %all-gather.21.cloned.1.call-start = ((), (), s32[]{:S(2)}) async-start(), calls=%async_computation.14 | async-start | bytes 7077888 | tf_op jit(solution)/shard_map/all_gather | solution.py:150
  1595.2 295.8 %copy-start.73 = (f32[2048]{0:T(1024)S(1)}, f32[2048]{0:T(1024)}, u32[]{:S(2)}) copy-start(f32[2048]{0:T(1024)} %param.41) | copy-start | bytes 24580
  1595.2 839.5 %all-reduce.99.cloned.1.call-start = ((), (), s32[]{:S(2)}) async-start(), calls=%async_computation.17 | async-start | bytes 16777216 | tf_op jit(solution)/shard_map/psum | solution.py:227
  2122.7 10.0 copy-start.108
  2122.7 10.0 copy-start.103
  2143.7 1777.1 %reduce-scatter.8.cloned.1.call-start = ((), (), s32[]{:S(2)}) async-start(), calls=%async_computation.15 | async-start | bytes 10485760 | tf_op jit(solution)/shard_map/reduce_scatter | solution.py:207
  2352.8 1776.5 %all-reduce.101.cloned.1.call-start = ((), (), s32[]{:S(2)}) async-start(), calls=%async_computation.18 | async-start | bytes 16777216 | tf_op jit(solution)/shard_map/psum | solution.py:277
  2434.7 9.0 copy-start.12
  2443.7 6.3 copy-start.26
  2449.7 10.2 copy-start.13
  3182.2 6.2 copy-start.34
  3207.2 6.1 copy-start.32
  3238.1 6.2 copy-start.30
  3280.8 6.2 copy-start.64
  3762.9 30.2 copy-start.96
  3762.9 30.2 copy-start.5
  3762.9 30.2 copy-start.70
  3762.9 30.3 copy-start.72
  3762.9 30.3 copy-start.75
  3762.9 30.3 copy-start.77
  3793.2 8.6 copy-start.7
  3793.2 8.6 copy-start.9
  3810.6 7.3 copy-start.85
  3810.6 7.3 copy-start.87
  3810.6 7.3 copy-start.89
  3810.6 7.3 copy-start.91
  3819.2 10.5 collective-permute-start.2
  3839.6 351.1 %all-reduce.103.cloned.1.call-start = ((), (), s32[]{:S(2)}) async-start(), calls=%async_computation.25 | async-start | bytes 2883584 | tf_op jit(solution)/shard_map/psum | solution.py:289
  3845.1 408.1 %reduce-scatter.14.cloned.1.call-start = ((), (), s32[]{:S(2)}) async-start(), calls=%async_computation.21 | async-start | bytes 6488064 | tf_op jit(solution)/shard_map/reduce_scatter | solution.py:284
  3854.6 461.5 %reduce-scatter.12.cloned.1.call-start = ((), (), s32[]{:S(2)}) async-start(), calls=%async_computation.20 | async-start | bytes 6488064 | tf_op jit(solution)/shard_map/reduce_scatter | solution.py:283
  3863.3 516.2 %reduce-scatter.10.cloned.1.call-start = ((), (), s32[]{:S(2)}) async-start(), calls=%async_computation.19 | async-start | bytes 6488064 | tf_op jit(solution)/shard_map/reduce_scatter | solution.py:282
  3872.4 603.4 %reduce-scatter.16.cloned.1.call-start = ((), (), s32[]{:S(2)}) async-start(), calls=%async_computation.22 | async-start | bytes 14155776 | tf_op jit(solution)/shard_map/reduce_scatter | solution.py:285
  3885.0 687.2 %reduce-scatter.18.cloned.1.call-start = ((), (), s32[]{:S(2)}) async-start(), calls=%async_computation.23 | async-start | bytes 14155776 | tf_op jit(solution)/shard_map/reduce_scatter | solution.py:286
  3897.6 771.1 %reduce-scatter.20.cloned.1.call-start = ((), (), s32[]{:S(2)}) async-start(), calls=%async_computation.24 | async-start | bytes 14155776 | tf_op jit(solution)/shard_map/reduce_scatter | solution.py:287
  3912.2 8.5 copy-start.97
  3924.4 213.0 %copy-start.94 = (f32[2048]{0:T(1024)S(1)}, f32[2048]{0:T(1024)}, u32[]{:S(2)}) copy-start(f32[2048]{0:T(1024)} %get-tuple-element.134) | copy-start | bytes 24580
  3924.4 238.4 %copy-start.83 = (f32[1024]{0:T(1024)S(1)}, f32[1024]{0:T(1024)}, u32[]{:S(2)}) copy-start(f32[1024]{0:T(1024)} %copy-done.82) | copy-start | bytes 12292
  (67 other events, 199.5 us)
Sparse Core Ops, SparseCore 0:
  9.6 83.4 all-gather.8
  95.0 30.1 all-gather.10
  127.1 35.1 all-gather.12
  164.0 31.6 all-gather.14
  1590.8 290.8 all-reduce.96
  1883.4 44.5 all-gather.16
  1929.8 45.5 all-gather.18
  1977.5 80.7 all-gather.22
  2060.2 44.0 all-gather.20
  2143.8 290.8 all-reduce.98
  2437.0 143.4 reduce-scatter.7
  3839.7 289.5 all-reduce.100
  4133.1 57.5 all-reduce.102
  4195.0 58.2 reduce-scatter.13
  4257.1 59.0 reduce-scatter.11
  4320.4 59.0 reduce-scatter.9
  4383.4 92.3 reduce-scatter.15
  4479.7 92.3 reduce-scatter.17
  4576.2 92.3 reduce-scatter.19
where the time goes:
time: 4710 us; the launch traced here: 4680 us
  local copies, waits for them, and re-layouts  2710 us (58%)
  waiting for transfers between devices  1400 us (30%)
  other arithmetic  315 us (7%)
  matrix products  186 us (4%)
    slice x62, local copies, waits for them, and re-layouts, shards(): lax.associative_scan(affine, (shifted, hidden_grad), axis=1, reverse=True)  809 us
    slice x58, local copies, waits for them, and re-layouts, shards(): lax.associative_scan(affine, (retain, inflow), axis=1)  752 us
    pad x36, local copies, waits for them, and re-layouts, shards(): lax.associative_scan(affine, (retain, inflow), axis=1)  508 us
    pad x36, local copies, waits for them, and re-layouts, shards(): lax.associative_scan(affine, (shifted, hidden_grad), axis=1, reverse=True)  504 us
    psum x1, waiting for transfers between devices, shards(): branch = lax.psum(contract_last(gated, fetched[2]), 'rep')  286 us
    psum x1, waiting for transfers between devices, shards(): normed_grad = lax.psum(normed_terms, 'rep')  205 us
    reduce_scatter x1, waiting for transfers between devices, shards(): lax.psum_scatter(feed_down_grad, ('seq', 'row'), scatter_dimension=0, til...  96.5 us
    reduce_scatter x1, waiting for transfers between devices, shards(): lax.psum_scatter(feed_up_grad, ('seq', 'row'), scatter_dimension=0, tiled...  96.4 us
  transfers between devices with their start and end apart: 22, of which 18 were waited for; matrix products, arithmetic and copies ran while one was open for 67% of the time, Pallas kernels for 0%

commit v1 on v0

--- a/solution.py
+++ b/solution.py
@@ -196,7 +196,9 @@
     block_windows = conv_input[:, None, -edge_width:]
     gated_f, gated_back = jax.vjp(output_gate, hidden, gate_branch)
     gated = gated_f.astype(jnp.bfloat16)
-    branch = lax.psum(contract_last(gated, fetched[2]), "rep")
+    own = contract_last(gated, fetched[2])
+    parts = lax.all_gather(own, "rep")
+    branch = jnp.sum(parts, axis=0)
     middle = input_float + branch
     normed_mid_f, norm_two_back = jax.vjp(rms_norm, middle, feed_gain)
     normed_mid = normed_mid_f.astype(jnp.bfloat16)

time: 4710 us -> 4980 us (1.057)
  waiting for transfers between devices: 1400 us -> 1650 us
    all_gather x0 -> x1, waiting for transfers between devices: none -> 557 us  [shards(): parts = lax.all_gather(own, 'rep')]
    psum x1 -> x0, waiting for transfers between devices: 286 us -> none  [shards(): branch = lax.psum(contract_last(gated, fetched[2]), 'rep')]
  transfers between devices with their start and end apart: 22 -> 22, of which waited for: 18 -> 18; matrix products, arithmetic and copies ran while one was open for 67% -> 64% of each run, Pallas kernels for 0% -> 0%
where the time goes in v1:
time: 4980 us; the launch traced here: 4950 us
  local copies, waits for them, and re-layouts  2710 us (54%)
  waiting for transfers between devices  1650 us (33%)
  other arithmetic  331 us (7%)
  matrix products  185 us (4%)
    slice x62, local copies, waits for them, and re-layouts, shards(): lax.associative_scan(affine, (shifted, hidden_grad), axis=1, reverse=True)  809 us
    slice x58, local copies, waits for them, and re-layouts, shards(): lax.associative_scan(affine, (retain, inflow), axis=1)  752 us
    all_gather x1, waiting for transfers between devices, shards(): parts = lax.all_gather(own, 'rep')  557 us
    pad x36, local copies, waits for them, and re-layouts, shards(): lax.associative_scan(affine, (retain, inflow), axis=1)  508 us
    pad x36, local copies, waits for them, and re-layouts, shards(): lax.associative_scan(affine, (shifted, hidden_grad), axis=1, reverse=True)  504 us
    psum x1, waiting for transfers between devices, shards(): normed_grad = lax.psum(normed_terms, 'rep')  205 us
  transfers between devices with their start and end apart: 22, of which 18 were waited for; matrix products, arithmetic and copies ran while one was open for 64% of the time, Pallas kernels for 0%

profile of v1, /device:TPU:0, one launch (start us, length us, event | category | flops | bytes accessed | tf_op | source)
XLA Modules:
  0.0 4947.7 jit_solution(8598455003491217840)
XLA Ops:
  20.5 72.6 %all-gather.11.cloned.1.call-done = bf16[1,1024,2048]{2,1,0:T(8,128)(2,1)} async-done(((bf16[1,1024,512]{2,1,0:T(8,128)(2,1)}), bf16[1,1024,2048]{2,1,0:T(8,128)(2,1)}) %all-gather.11.cloned.1.call-update) | async-done | bytes 4194320 | tf_op jit(solution)/shard_map/all_gather | solution.py:141
  96.2 29.0 all-gather.13.cloned.1.call-done
  135.3 27.0 all-gather.15.cloned.1.call-done
  181.5 50.8 %slice.699 = f32[1,512,704]{1,2,0:T(8,128)} slice(f32[1,1024,704]{1,2,0:T(8,128)S(1)} %get-tuple-element.180), slice={[0:1:1], [1:1024:2], [0:704:1]} | slice | bytes 2883584 | tf_op jit(solution)/shard_map/slice | solution.py:185
  232.3 50.7 %slice.703 = f32[1,512,704]{1,2,0:T(8,128)} slice(f32[1,1024,704]{1,2,0:T(8,128)S(1)} %get-tuple-element.180), slice={[0:1:1], [0:1023:2], [0:704:1]} | slice | bytes 2883584 | tf_op jit(solution)/shard_map/slice | solution.py:185
  283.0 51.6 %slice.700 = f32[1,512,704]{1,2,0:T(8,128)} slice(f32[1,1024,704]{1,2,0:T(8,128)} %get-tuple-element.181), slice={[0:1:1], [0:1023:2], [0:704:1]} | slice | bytes 2883584 | tf_op jit(solution)/shard_map/slice | solution.py:185
  334.7 51.3 %slice.701 = f32[1,512,704]{1,2,0:T(8,128)} slice(f32[1,1024,704]{1,2,0:T(8,128)} %get-tuple-element.181), slice={[0:1:1], [1:1024:2], [0:704:1]} | slice | bytes 2883584 | tf_op jit(solution)/shard_map/slice | solution.py:185
  390.9 28.3 slice.706
  419.2 28.3 slice.707
  447.5 28.5 slice.705
  476.0 28.3 slice.709
  541.0 17.0 slice.711
  795.4 28.2 slice.704
  823.6 28.4 slice.769
  855.5 50.7 %slice.698 = f32[1,511,704]{1,2,0:T(8,128)} slice(f32[1,1024,704]{1,2,0:T(8,128)S(1)} %get-tuple-element.180), slice={[0:1:1], [2:1024:2], [0:704:1]} | slice | bytes 2877952 | tf_op jit(solution)/shard_map/slice | solution.py:185
  906.2 51.2 %slice.771 = f32[1,511,704]{1,2,0:T(8,128)} slice(f32[1,1024,704]{1,2,0:T(8,128)} %get-tuple-element.181), slice={[0:1:1], [2:1024:2], [0:704:1]} | slice | bytes 2877952 | tf_op jit(solution)/shard_map/slice | solution.py:185
  1198.9 28.7 pad.306
  1227.6 28.7 pad.307
  1256.3 28.9 pad.287
  1287.5 28.6 pad.286
  1326.0 57.0 %pad.308 = f32[1,1024,704]{1,2,0:T(8,128)} pad(f32[1,512,704]{1,2,0:T(8,128)} %pad_maximum_fusion.1, f32[]{:T(128)} %constant.20.clone.1), padding=0_0_0x0_1_1x0_0_0 | pad | bytes 4325380 | tf_op jit(solution)/shard_map/pad | solution.py:185
  1383.0 57.2 %pad.309 = f32[1,1024,704]{1,2,0:T(8,128)} pad(f32[1,512,704]{1,2,0:T(8,128)} %add.768, f32[]{:T(128)} %constant.20.clone.1), padding=0_0_0x1_0_1x0_0_0 | pad | bytes 4325380 | tf_op jit(solution)/shard_map/pad | solution.py:185
  1446.4 57.1 %pad.288 = f32[1,1024,704]{1,2,0:T(8,128)} pad(f32[1,512,704]{1,2,0:T(8,128)} %pad_maximum_fusion, f32[]{:T(128)} %constant.20.clone.1), padding=0_0_0x0_1_1x0_0_0 | pad | bytes 4325380 | tf_op jit(solution)/shard_map/pad | solution.py:185
  1503.4 57.3 %pad.289 = f32[1,1024,704]{1,2,0:T(8,128)} pad(f32[1,512,704]{1,2,0:T(8,128)} %add.757, f32[]{:T(128)} %constant.20.clone.1), padding=0_0_0x1_0_1x0_0_0 | pad | bytes 4325380 | tf_op jit(solution)/shard_map/pad | solution.py:185
  1594.0 556.9 %all-gather.27.cloned.1.call-done = f32[4096,2048]{1,0:T(8,128)} async-done(((f32[1024,2048]{1,0:T(8,128)}), f32[4096,2048]{1,0:T(8,128)}) %all-gather.27.cloned.1.call-update) | async-done | bytes 33554448 | tf_op jit(solution)/shard_map/all_gather | solution.py:200
  2150.9 16.9 reduce.13
  2208.1 35.7 all-gather.21.cloned.1.call-done
  2255.6 71.2 %all-gather.25.cloned.1.call-done = bf16[1,1024,2048]{2,1,0:T(8,128)(2,1)} async-done(((bf16[1,1024,512]{2,1,0:T(8,128)(2,1)}), bf16[1,1024,2048]{2,1,0:T(8,128)(2,1)}) %all-gather.25.cloned.1.call-update) | async-done | bytes 4194320 | tf_op jit(solution)/shard_map/all_gather | solution.py:142
  2326.8 46.0 all-gather.23.cloned.1.call-done
  2372.8 18.5 multiply_convert_fusion.2
  2414.5 51.4 %slice.798 = f32[1,512,704]{1,2,0:T(8,128)} slice(f32[1,1024,704]{1,2,0:T(8,128)} %concatenate.160), slice={[0:1:1], [0:1023:2], [0:704:1]} | slice | bytes 2883584 | tf_op jit(solution)/shard_map/slice | solution.py:240
  2465.9 51.3 %slice.805 = f32[1,512,704]{1,2,0:T(8,128)} slice(f32[1,1024,704]{1,2,0:T(8,128)} %concatenate.160), slice={[0:1:1], [1:1024:2], [0:704:1]} | slice | bytes 2883584 | tf_op jit(solution)/shard_map/slice | solution.py:240
  2517.2 51.3 %slice.796 = f32[1,511,704]{1,2,0:T(8,128)} slice(f32[1,1024,704]{1,2,0:T(8,128)} %concatenate.160), slice={[0:1:1], [1:1022:2], [0:704:1]} | slice | bytes 2877952 | tf_op jit(solution)/shard_map/slice | solution.py:240
  2621.1 81.8 %all-reduce.96.cloned.1.call-done = f32[1,1024,2048]{2,1,0:T(8,128)} async-done(((f32[1,1024,2048]{2,1,0:T(8,128)}), f32[1,1024,2048]{2,1,0:T(8,128)}) %all-reduce.96.cloned.1.call-update) | async-done | bytes 8388624 | tf_op jit(solution)/shard_map/psum | solution.py:229
  2730.6 51.3 %slice.800 = f32[1,512,704]{1,2,0:T(8,128)} slice(f32[1,1024,704]{1,2,0:T(8,128)} %multiply_bitcast_fusion), slice={[0:1:1], [1:1024:2], [0:704:1]} | slice | bytes 2883584 | tf_op jit(solution)/shard_map/slice | solution.py:240
  2781.9 51.4 %slice.802 = f32[1,512,704]{1,2,0:T(8,128)} slice(f32[1,1024,704]{1,2,0:T(8,128)} %multiply_bitcast_fusion), slice={[0:1:1], [0:1023:2], [0:704:1]} | slice | bytes 2883584 | tf_op jit(solution)/shard_map/slice | solution.py:240
  2864.8 28.3 slice.809
  2893.1 28.3 slice.810
  2921.4 28.3 slice.808
  2949.7 28.5 slice.812
  3031.8 17.2 slice.818
  3227.8 16.9 slice.813
  3265.0 28.2 slice.807
  3293.2 28.6 slice.872
  3325.3 51.3 %slice.874 = f32[1,511,704]{1,2,0:T(8,128)} slice(f32[1,1024,704]{1,2,0:T(8,128)} %multiply_bitcast_fusion), slice={[0:1:1], [1:1022:2], [0:704:1]} | slice | bytes 2877952 | tf_op jit(solution)/shard_map/slice | solution.py:240
  3623.2 28.9 pad.326
  3652.1 28.7 pad.327
  3684.0 57.2 %pad.329 = f32[1,1024,704]{1,2,0:T(8,128)} pad(f32[1,512,704]{1,2,0:T(8,128)} %add.810, f32[]{:T(128)} %constant.20.clone.1), padding=0_0_0x1_0_1x0_0_0 | pad | bytes 4325380 | tf_op jit(solution)/shard_map/pad | solution.py:240
  3743.5 28.7 pad.346
  3772.2 28.6 pad.347
  3822.9 57.1 %pad.328 = f32[1,1024,704]{1,2,0:T(8,128)} pad(f32[1,512,704]{1,2,0:T(8,128)} %pad_maximum_fusion.2, f32[]{:T(128)} %constant.20.clone.1), padding=0_0_0x0_1_1x0_0_0 | pad | bytes 4325380 | tf_op jit(solution)/shard_map/pad | solution.py:240
  3888.3 52.7 %pad.349 = f32[1,1024,704]{1,2,0:T(8,128)S(1)} pad(f32[1,512,704]{1,2,0:T(8,128)} %add.821, f32[]{:T(128)} %constant.20.clone.1), padding=0_0_0x1_0_1x0_0_0 | pad | bytes 4325380 | tf_op jit(solution)/shard_map/pad | solution.py:240
  3943.9 57.2 %pad.348 = f32[1,1024,704]{1,2,0:T(8,128)} pad(f32[1,512,704]{1,2,0:T(8,128)} %concatenate.178, f32[]{:T(128)} %constant.20.clone.1), padding=0_0_0x0_1_1x0_0_0 | pad | bytes 4325380 | tf_op jit(solution)/shard_map/pad | solution.py:240
  4005.1 25.7 rev.5
  4030.8 25.9 rev.4
  4192.5 204.7 %all-reduce.98.cloned.1.call-done = f32[1,1024,2048]{2,1,0:T(8,128)} async-done(((f32[1,1024,2048]{2,1,0:T(8,128)}), f32[1,1024,2048]{2,1,0:T(8,128)}) %all-reduce.98.cloned.1.call-update) | async-done | bytes 8388624 | tf_op jit(solution)/shard_map/psum | solution.py:279
  4405.4 25.4 all-reduce.90
  4435.2 23.5 all-reduce.100.cloned.1.call-done
  4458.7 62.5 %reduce-scatter.14.cloned.1.call-done = f32[256,704]{0,1:T(8,128)} async-done(((f32[2048,704]{0,1:T(8,128)}), f32[256,704]{0,1:T(8,128)}) %reduce-scatter.14.cloned.1.call-update) | async-done | bytes 720912 | tf_op jit(solution)/shard_map/reduce_scatter | solution.py:286
  4521.2 62.9 %reduce-scatter.12.cloned.1.call-done = f32[256,704]{0,1:T(8,128)} async-done(((f32[2048,704]{0,1:T(8,128)}), f32[256,704]{0,1:T(8,128)}) %reduce-scatter.12.cloned.1.call-update) | async-done | bytes 720912 | tf_op jit(solution)/shard_map/reduce_scatter | solution.py:285
  4584.1 63.3 %reduce-scatter.10.cloned.1.call-done = f32[256,704]{0,1:T(8,128)} async-done(((f32[2048,704]{0,1:T(8,128)}), f32[256,704]{0,1:T(8,128)}) %reduce-scatter.10.cloned.1.call-update) | async-done | bytes 720912 | tf_op jit(solution)/shard_map/reduce_scatter | solution.py:284
  4647.5 96.3 %reduce-scatter.16.cloned.1.call-done = f32[256,1536]{1,0:T(8,128)} async-done(((f32[2048,1536]{1,0:T(8,128)}), f32[256,1536]{1,0:T(8,128)}) %reduce-scatter.16.cloned.1.call-update) | async-done | bytes 1572880 | tf_op jit(solution)/shard_map/reduce_scatter | solution.py:287
  4743.8 96.4 %reduce-scatter.18.cloned.1.call-done = f32[256,1536]{1,0:T(8,128)} async-done(((f32[2048,1536]{1,0:T(8,128)}), f32[256,1536]{1,0:T(8,128)}) %reduce-scatter.18.cloned.1.call-update) | async-done | bytes 1572880 | tf_op jit(solution)/shard_map/reduce_scatter | solution.py:288
  4840.2 96.5 %reduce-scatter.20.cloned.1.call-done = f32[256,1536]{1,0:T(8,128)} async-done(((f32[2048,1536]{1,0:T(8,128)}), f32[256,1536]{1,0:T(8,128)}) %reduce-scatter.20.cloned.1.call-update) | async-done | bytes 1572880 | tf_op jit(solution)/shard_map/reduce_scatter | solution.py:289
  (643 shorter events, 1504.6 us)
Async XLA Ops:
  7.2 167.4 %copy-start = (bf16[4,176,176]{2,1,0:T(8,128)(2,1)S(1)}, bf16[4,176,176]{2,1,0:T(8,128)(2,1)}, u32[]{:S(2)}) copy-start(bf16[4,176,176]{2,1,0:T(8,128)(2,1)} %param.36) | copy-start | bytes 743428
  7.2 85.9 %all-gather.11.cloned.1.call-start = ((), (), s32[]{:S(2)}) async-start(), calls=%async_computation.7 | async-start | bytes 5242880 | tf_op jit(solution)/shard_map/all_gather | solution.py:141
  7.9 117.3 %copy-start.98 = (f32[2048]{0:T(1024)S(1)}, f32[2048]{0:T(1024)}, u32[]{:S(2)}) copy-start(f32[2048]{0:T(1024)} %param.40) | copy-start | bytes 24580
  8.0 117.3 %all-gather.13.cloned.1.call-start = ((), (), s32[]{:S(2)}) async-start(), calls=%async_computation.8 | async-start | bytes 3244032 | tf_op jit(solution)/shard_map/all_gather | solution.py:145
  8.7 153.6 %all-gather.15.cloned.1.call-start = ((), (), s32[]{:S(2)}) async-start(), calls=%async_computation.9 | async-start | bytes 3244032 | tf_op jit(solution)/shard_map/all_gather | solution.py:146
  9.4 1570.8 %all-gather.17.cloned.1.call-start = ((), (), s32[]{:S(2)}) async-start(), calls=%async_computation.10 | async-start | bytes 3244032 | tf_op jit(solution)/shard_map/all_gather | solution.py:147
  10.2 8.6 collective-permute-start.1
  15.1 2135.8 %all-gather.27.cloned.1.call-start = ((), (), s32[]{:S(2)}) async-start(), calls=%async_computation.24 | async-start | bytes 41943040 | tf_op jit(solution)/shard_map/all_gather | solution.py:200
  18.1 152.9 %copy-start.84 = (f32[704]{0:T(1024)}, f32[704]{0:T(1024)S(1)}, u32[]{:S(2)}) copy-start(f32[704]{0:T(1024)S(1)} %get-tuple-element.143) | copy-start | bytes 8452
  18.1 152.9 %copy-start.86 = (f32[704]{0:T(1024)}, f32[704]{0:T(1024)S(1)}, u32[]{:S(2)}) copy-start(f32[704]{0:T(1024)S(1)} %get-tuple-element.144) | copy-start | bytes 8452
  18.1 152.9 %copy-start.88 = (f32[704]{0:T(1024)}, f32[704]{0:T(1024)S(1)}, u32[]{:S(2)}) copy-start(f32[704]{0:T(1024)S(1)} %get-tuple-element.145) | copy-start | bytes 8452
  18.1 152.9 %copy-start.90 = (f32[704]{0:T(1024)}, f32[704]{0:T(1024)S(1)}, u32[]{:S(2)}) copy-start(f32[704]{0:T(1024)S(1)} %get-tuple-element.146) | copy-start | bytes 8452
  18.8 157.6 %copy-start.71 = (f32[704]{0:T(1024)}, f32[704]{0:T(1024)S(1)}, u32[]{:S(2)}) copy-start(f32[704]{0:T(1024)S(1)} %fusion.79) | copy-start | bytes 8452
  20.5 150.6 %copy-start.78 = (f32[1,1024]{1,0:T(1,128)}, f32[1,1024]{1,0:T(1,128)S(1)}, u32[]{:S(2)}) copy-start(f32[1,1024]{1,0:T(1,128)S(1)} %get-tuple-element.273) | copy-start | bytes 12292
  20.5 150.6 %copy-start.80 = (f32[1,1024]{1,0:T(1,128)}, f32[1,1024]{1,0:T(1,128)S(1)}, u32[]{:S(2)}) copy-start(f32[1,1024]{1,0:T(1,128)S(1)} %get-tuple-element.274) | copy-start | bytes 12292
  20.5 155.9 %copy-start.69 = (f32[1,1024]{1,0:T(1,128)}, f32[1,1024]{1,0:T(1,128)S(1)}, u32[]{:S(2)}) copy-start(f32[1,1024]{1,0:T(1,128)S(1)} %get-tuple-element.272) | copy-start | bytes 12292
  96.2 35.4 copy-start.82
  96.2 66.1 %copy-start.92 = (f32[1024]{0:T(1024)}, f32[1024]{0:T(1024)S(1)}, u32[]{:S(2)}) copy-start(f32[1024]{0:T(1024)S(1)} %fusion.80) | copy-start | bytes 12292
  132.3 37.8 collective-permute-start
  1026.2 6.2 copy-start.33
  1051.2 6.2 copy-start.31
  1082.0 6.2 copy-start.29
  1503.4 69.1 %copy-start.102 = (f32[1,704]{1,0:T(1,128)S(1)}, f32[1,704]{1,0:T(1,128)}, u32[]{:S(2)}) copy-start(f32[1,704]{1,0:T(1,128)} %param.25) | copy-start | bytes 8452
  1589.4 607.0 %all-gather.19.cloned.1.call-start = ((), (), s32[]{:S(2)}) async-start(), calls=%async_computation.11 | async-start | bytes 7077888 | tf_op jit(solution)/shard_map/all_gather | solution.py:148
  1589.9 653.9 %all-gather.21.cloned.1.call-start = ((), (), s32[]{:S(2)}) async-start(), calls=%async_computation.12 | async-start | bytes 7077888 | tf_op jit(solution)/shard_map/all_gather | solution.py:149
  1590.7 736.1 %all-gather.25.cloned.1.call-start = ((), (), s32[]{:S(2)}) async-start(), calls=%async_computation.15 | async-start | bytes 5242880 | tf_op jit(solution)/shard_map/all_gather | solution.py:142
  1593.2 779.6 %all-gather.23.cloned.1.call-start = ((), (), s32[]{:S(2)}) async-start(), calls=%async_computation.13 | async-start | bytes 7077888 | tf_op jit(solution)/shard_map/all_gather | solution.py:150
  1593.9 1108.9 %all-reduce.96.cloned.1.call-start = ((), (), s32[]{:S(2)}) async-start(), calls=%async_computation.16 | async-start | bytes 16777216 | tf_op jit(solution)/shard_map/psum | solution.py:229
  2167.9 9.6 copy-start.73
  2391.2 10.0 copy-start.108
  2391.2 10.0 copy-start.103
  2411.9 1777.0 %reduce-scatter.8.cloned.1.call-start = ((), (), s32[]{:S(2)}) async-start(), calls=%async_computation.14 | async-start | bytes 10485760 | tf_op jit(solution)/shard_map/reduce_scatter | solution.py:209
  2621.0 1776.2 %all-reduce.98.cloned.1.call-start = ((), (), s32[]{:S(2)}) async-start(), calls=%async_computation.17 | async-start | bytes 16777216 | tf_op jit(solution)/shard_map/psum | solution.py:279
  2702.9 9.0 copy-start.12
  2711.8 6.3 copy-start.26
  2717.9 10.2 copy-start.13
  3450.4 6.2 copy-start.34
  3506.2 6.2 copy-start.30
  3549.0 6.2 copy-start.64
  4030.8 30.3 copy-start.96
  4030.8 30.3 copy-start.5
  4030.8 30.3 copy-start.70
  4030.8 30.3 copy-start.72
  4030.8 30.3 copy-start.75
  4030.8 30.3 copy-start.77
  4061.1 8.6 copy-start.7
  4061.1 8.6 copy-start.9
  4078.6 7.3 copy-start.85
  4078.6 7.3 copy-start.87
  4078.6 7.3 copy-start.89
  4078.6 7.3 copy-start.91
  4087.2 10.5 collective-permute-start.2
  4091.9 6.2 copy-start.62
  4091.9 6.2 copy-start.104
  4107.6 351.1 %all-reduce.100.cloned.1.call-start = ((), (), s32[]{:S(2)}) async-start(), calls=%async_computation.25 | async-start | bytes 2883584 | tf_op jit(solution)/shard_map/psum | solution.py:291
  4113.1 408.1 %reduce-scatter.14.cloned.1.call-start = ((), (), s32[]{:S(2)}) async-start(), calls=%async_computation.20 | async-start | bytes 6488064 | tf_op jit(solution)/shard_map/reduce_scatter | solution.py:286
  4122.6 461.5 %reduce-scatter.12.cloned.1.call-start = ((), (), s32[]{:S(2)}) async-start(), calls=%async_computation.19 | async-start | bytes 6488064 | tf_op jit(solution)/shard_map/reduce_scatter | solution.py:285
  4131.3 516.1 %reduce-scatter.10.cloned.1.call-start = ((), (), s32[]{:S(2)}) async-start(), calls=%async_computation.18 | async-start | bytes 6488064 | tf_op jit(solution)/shard_map/reduce_scatter | solution.py:284
  4140.4 603.4 %reduce-scatter.16.cloned.1.call-start = ((), (), s32[]{:S(2)}) async-start(), calls=%async_computation.21 | async-start | bytes 14155776 | tf_op jit(solution)/shard_map/reduce_scatter | solution.py:287
  4153.0 687.2 %reduce-scatter.18.cloned.1.call-start = ((), (), s32[]{:S(2)}) async-start(), calls=%async_computation.22 | async-start | bytes 14155776 | tf_op jit(solution)/shard_map/reduce_scatter | solution.py:288
  4165.6 771.1 %reduce-scatter.20.cloned.1.call-start = ((), (), s32[]{:S(2)}) async-start(), calls=%async_computation.23 | async-start | bytes 14155776 | tf_op jit(solution)/shard_map/reduce_scatter | solution.py:289
  4180.3 8.5 copy-start.97
  4192.5 212.9 %copy-start.94 = (f32[2048]{0:T(1024)S(1)}, f32[2048]{0:T(1024)}, u32[]{:S(2)}) copy-start(f32[2048]{0:T(1024)} %get-tuple-element.134) | copy-start | bytes 24580
  4192.5 238.3 %copy-start.83 = (f32[1024]{0:T(1024)S(1)}, f32[1024]{0:T(1024)}, u32[]{:S(2)}) copy-start(f32[1024]{0:T(1024)} %copy-done.82) | copy-start | bytes 12292
  (67 other events, 199.7 us)
Sparse Core Ops, SparseCore 0:
  9.6 83.4 all-gather.10
  95.0 30.1 all-gather.12
  127.1 35.1 all-gather.14
  164.0 31.6 all-gather.16
  1589.5 561.3 all-gather.26
  2152.7 43.7 all-gather.18
  2198.3 45.5 all-gather.20
  2246.0 80.7 all-gather.24
  2328.7 44.0 all-gather.22
  2412.0 290.8 all-reduce.95
  2705.2 143.4 reduce-scatter.7
  4107.7 289.5 all-reduce.97
  4401.1 57.5 all-reduce.99
  4463.0 58.2 reduce-scatter.13
  4525.1 59.0 reduce-scatter.11
  4588.4 59.0 reduce-scatter.9
  4651.4 92.3 reduce-scatter.15
  4747.7 92.3 reduce-scatter.17
  4844.2 92.3 reduce-scatter.19
